TPU v7x, 32 devices: a whole 2x2x4 slice. The times are simulated.
32 devices in a mesh: row: 4 (over x, core), col: 8 (over z, y).
Axes of the slice: x: 2, y: 2, z: 4, core: 2. Of those that a mesh axis runs over, the one named last changes fastest.
Arguments:
- iterate: bfloat16 [4096, 8192], P('row', 'col'), may hold values from -0.5 to 0.5, as said below
Outputs:
- update: float32 [4096, 8192], P('row', 'col')
Inputs may be any that keep to these rules, and one draw needn't show every extreme that they name: One iterate of the orthogonalization.
All inputs are finite; a program needn't handle non-finite values.
Results may differ from a plain program's by a relative error of at most 0.0041.
Values may be sent and summed in bfloat16 or wider, within the bound.
A program may use at most 64 MiB of HBM per device.

v0:
```python
import math
import jax
import jax.numpy as jnp
from jax import lax
from jax.sharding import PartitionSpec as P

COLS = 8192
coef_a = 3.4445
coef_b = -4.775
coef_c = 2.0315


def per_device(iterate):
    cols_x = lax.all_gather(iterate, "row", axis=0, tiled=True)
    mirrored = lax.psum_scatter(
        lax.dot_general(
            cols_x, iterate, (((1,), (1,)), ((), ())), preferred_element_type=jnp.float32
        ),
        "col",
        scatter_dimension=0,
        tiled=True,
    )
    gram_block = mirrored.T.astype(jnp.bfloat16)
    gram_cols = lax.all_gather(gram_block, "row", axis=0, tiled=True)
    lower = gram_cols
    square = jnp.dot(
        lax.all_gather(gram_block, "col", axis=1, tiled=True),
        lower,
        preferred_element_type=jnp.float32,
    )
    poly = (coef_b * gram_block.astype(jnp.float32) + coef_c * square).astype(jnp.bfloat16)
    lower = cols_x
    mixed = jnp.dot(
        lax.all_gather(poly, "col", axis=1, tiled=True), lower, preferred_element_type=jnp.float32
    )
    return math.sqrt(COLS) * (coef_a * iterate.astype(jnp.float32) + mixed)


def solution(mesh):
    placed = (P("row", "col"),)
    return jax.shard_map(
        per_device, mesh=mesh, in_specs=placed, out_specs=P("row", "col"), check_vma=False
    )
```

profile of v0, /device:TPU:0, one launch (start us, length us, event | category | flops | bytes accessed | tf_op | source)
XLA Modules:
  0.0 684.1 jit_solution(4347285785540661950)
XLA Ops:
  6.5 0.0 all-gather.5.cloned.1.call-start
  6.5 0.7 all-gather.5.cloned.1.call-update
  7.3 0.0 reduce-scatter.2.cloned.1.call-start
  7.3 62.6 %all-gather.5.cloned.1.call-done = bf16[4096,1024]{1,0:T(8,128)(2,1)} async-done(((bf16[1024,1024]{1,0:T(8,128)(2,1)}), bf16[4096,1024]{1,0:T(8,128)(2,1)}) %all-gather.5.cloned.1.call-update) | async-done | bytes 8388624 | tf_op jit(solution)/shard_map/all_gather | solution.py:14
  69.9 16.1 %fusion = f32[4096,1024]{1,0:T(8,128)} fusion(bf16[4096,1024]{1,0:T(8,128)(2,1)} %all-gather.5.cloned.1.call-done, bf16[1024,1024]{1,0:T(8,128)(2,1)} %param.1), kind=kOutput, calls=%fused_computation.3 | convolution fusion | flops 8589934592 | bytes 27262976 | tf_op jit(solution)/shard_map/dot_general | solution.py:16
  86.1 0.0 reduce-scatter.2.cloned.1.call-update
  86.1 0.0 all-gather.9.cloned.1.call-start
  86.1 280.3 %reduce-scatter.2.cloned.1.call-done = f32[512,1024]{1,0:T(8,128)} async-done(((f32[4096,1024]{1,0:T(8,128)}), f32[512,1024]{1,0:T(8,128)}) %reduce-scatter.2.cloned.1.call-update) | async-done | bytes 2097168 | tf_op jit(solution)/shard_map/reduce_scatter | solution.py:15
  366.5 2.7 convert_bitcast_fusion
  369.2 0.0 all-gather.9.cloned.1.call-update
  369.2 0.0 all-gather.7.cloned.1.call-start
  369.2 0.5 all-gather.7.cloned.1.call-update
  369.8 0.0 copy-start
  369.8 0.0 all-gather.11.cloned.1.call-start
  369.8 33.1 %all-gather.9.cloned.1.call-done = bf16[4096,512]{0,1:T(8,128)(2,1)} async-done(((bf16[1024,512]{0,1:T(8,128)(2,1)}), bf16[4096,512]{0,1:T(8,128)(2,1)}) %all-gather.9.cloned.1.call-update) | async-done | bytes 4194320 | tf_op jit(solution)/shard_map/all_gather | solution.py:24
  402.9 126.5 %all-gather.7.cloned.1.call-done = bf16[1024,4096]{0,1:T(8,128)(2,1)} async-done(((bf16[1024,512]{0,1:T(8,128)(2,1)}), bf16[1024,4096]{0,1:T(8,128)(2,1)}) %all-gather.7.cloned.1.call-update) | async-done | bytes 8388624 | tf_op jit(solution)/shard_map/all_gather | solution.py:27
  529.4 10.3 %add_convert_fusion = bf16[1024,512]{0,1:T(8,128)(2,1)} fusion(bf16[1024,512]{0,1:T(8,128)(2,1)} %convert_bitcast_fusion, bf16[4096,512]{0,1:T(8,128)(2,1)} %all-gather.9.cloned.1.call-done, bf16[1024,4096]{0,1:T(8,128)(2,1)} %all-gather.7.cloned.1.call-done), kind=kOutput, calls=%fused_computation.1 | convolution fusion | flops 4297588736 | bytes 14680064 | tf_op jit(solution)/shard_map/dot_general | solution.py:26
  539.7 0.0 all-gather.11.cloned.1.call-update
  539.7 122.8 %all-gather.11.cloned.1.call-done = bf16[1024,4096]{0,1:T(8,128)(2,1)} async-done(((bf16[1024,512]{0,1:T(8,128)(2,1)}), bf16[1024,4096]{0,1:T(8,128)(2,1)}) %all-gather.11.cloned.1.call-update) | async-done | bytes 8388624 | tf_op jit(solution)/shard_map/all_gather | solution.py:34
  662.5 0.0 copy-done
  662.5 15.1 %add_multiply_fusion = f32[1024,1024]{1,0:T(8,128)} fusion(bf16[1024,1024]{1,0:T(8,128)(2,1)S(1)} %copy-done, bf16[1024,4096]{0,1:T(8,128)(2,1)} %all-gather.11.cloned.1.call-done, bf16[4096,1024]{1,0:T(8,128)(2,1)} %all-gather.5.cloned.1.call-done), kind=kOutput, calls=%fused_computation | convolution fusion | flops 8594128896 | bytes 23068672 | tf_op jit(solution)/shard_map/dot_general | solution.py:33
Async XLA Ops:
  6.5 63.4 %all-gather.5.cloned.1.call-start = ((), (), s32[]{:S(2)}) async-start(), calls=%async_computation.1 | async-start | bytes 10485760 | tf_op jit(solution)/shard_map/all_gather | solution.py:14
  7.3 359.2 %reduce-scatter.2.cloned.1.call-start = ((), (), s32[]{:S(2)}) async-start(), calls=%async_computation.2 | async-start | bytes 18874368 | tf_op jit(solution)/shard_map/reduce_scatter | solution.py:15
  86.1 316.8 %all-gather.9.cloned.1.call-start = ((), (), s32[]{:S(2)}) async-start(), calls=%async_computation.4 | async-start | bytes 5242880 | tf_op jit(solution)/shard_map/all_gather | solution.py:24
  369.2 160.2 %all-gather.7.cloned.1.call-start = ((), (), s32[]{:S(2)}) async-start(), calls=%async_computation.3 | async-start | bytes 9437184 | tf_op jit(solution)/shard_map/all_gather | solution.py:27
  369.8 292.8 %copy-start = (bf16[1024,1024]{1,0:T(8,128)(2,1)S(1)}, bf16[1024,1024]{1,0:T(8,128)(2,1)}, u32[]{:S(2)}) copy-start(bf16[1024,1024]{1,0:T(8,128)(2,1)} %param.1) | copy-start | bytes 6291460
  369.8 292.7 %all-gather.11.cloned.1.call-start = ((), (), s32[]{:S(2)}) async-start(), calls=%async_computation.5 | async-start | bytes 9437184 | tf_op jit(solution)/shard_map/all_gather | solution.py:34
Sparse Core Ops, SparseCore 0:
  8.9 60.9 all-gather.4
  86.2 280.2 reduce-scatter.1
  369.3 33.5 all-gather.8
  404.9 124.4 all-gather.6
  539.8 122.6 all-gather.10
where the time goes:
time: 684 us
  waiting for transfers between devices  627 us (92%)
  matrix products  41.5 us (6%)
  between operations  13.1 us (2%)
    reduce_scatter x1, waiting for transfers between devices, per_device(): lax.psum_scatter(lax.dot_general(cols_x, iterate, (((1,), (1,)), ((), ())...  280 us
    all_gather x1, waiting for transfers between devices, per_device(): lax.all_gather(gram_block, 'col', axis=1, tiled=True)  126 us
    all_gather x1, waiting for transfers between devices, per_device(): lax.all_gather(poly, 'col', axis=1, tiled=True)  123 us
    all_gather x1, waiting for transfers between devices, per_device(): cols_x = lax.all_gather(iterate, 'row', axis=0, tiled=True)  62.6 us
    all_gather x1, waiting for transfers between devices, per_device(): gram_cols = lax.all_gather(gram_block, 'row', axis=0, tiled=True)  33.1 us
    dot_general x1, matrix products, per_device(): lax.dot_general(cols_x, iterate, (((1,), (1,)), ((), ())), preferred_elem...  16.1 us
    dot_general x1, matrix products, per_device(): jnp.dot(lax.all_gather(poly, 'col', axis=1, tiled=True), lower, preferred...  15.1 us
  transfers between devices with their start and end apart: 5, of which 5 were waited for; matrix products, arithmetic and copies ran while one was open for 0% of the time, Pallas kernels for 0%

commit v1 on v0

--- a/solution.py
+++ b/solution.py
@@ -11,7 +11,13 @@
 
 
 def per_device(iterate):
-    cols_x = lax.all_gather(iterate, "row", axis=0, tiled=True)
+    size = lax.axis_size("row")
+    held, blocks = (iterate, [iterate])
+    for _ in range(size - 1):
+        held = lax.ppermute(held, "row", [(i, (i + 1) % size) for i in range(size)])
+        blocks.insert(0, held)
+    merged = jnp.concatenate(blocks, axis=0)
+    cols_x = jnp.roll(merged, (lax.axis_index("row") + 1) * iterate.shape[0], axis=0)
     mirrored = lax.psum_scatter(
         lax.dot_general(
             cols_x, iterate, (((1,), (1,)), ((), ())), preferred_element_type=jnp.float32

time: 684 us -> 711 us (1.039)
  waiting for transfers between devices: 627 us -> 643 us
  local copies, waits for them, and re-layouts: 0.01 us -> 14.8 us
    ppermute x0 -> x3, waiting for transfers between devices: none -> 77.2 us  [per_device(): held = lax.ppermute(held, 'row', [(i, (i + 1) % size) for i in range(size)])]
    all_gather x1 -> x0, waiting for transfers between devices: 62.6 us -> none  [per_device(): cols_x = lax.all_gather(iterate, 'row', axis=0, tiled=True)]
    unnamed x2 -> x15, local copies, waits for them, and re-layouts: 0.01 us -> 14.6 us
  transfers between devices with their start and end apart: 5 -> 7, of which waited for: 5 -> 7; matrix products, arithmetic and copies ran while one was open for 0% -> 0% of each run, Pallas kernels for 0% -> 0%
where the time goes in v1:
time: 711 us
  waiting for transfers between devices  643 us (90%)
  matrix products  37.2 us (5%)
  local copies, waits for them, and re-layouts  14.8 us (2%)
  between operations  13.2 us (2%)
    reduce_scatter x1, waiting for transfers between devices, per_device(): lax.psum_scatter(lax.dot_general(cols_x, iterate, (((1,), (1,)), ((), ())...  282 us
    all_gather x1, waiting for transfers between devices, per_device(): lax.all_gather(gram_block, 'col', axis=1, tiled=True)  127 us
    all_gather x1, waiting for transfers between devices, per_device(): lax.all_gather(poly, 'col', axis=1, tiled=True)  123 us
    ppermute x3, waiting for transfers between devices, per_device(): held = lax.ppermute(held, 'row', [(i, (i + 1) % size) for i in range(size)])  77.2 us
    all_gather x1, waiting for transfers between devices, per_device(): gram_cols = lax.all_gather(gram_block, 'row', axis=0, tiled=True)  32.9 us
    dot_general x1, matrix products, per_device(): jnp.dot(lax.all_gather(poly, 'col', axis=1, tiled=True), lower, preferred...  15.1 us
    unnamed x15, local copies, waits for them, and re-layouts  14.6 us
  transfers between devices with their start and end apart: 7, of which 7 were waited for; matrix products, arithmetic and copies ran while one was open for 0% of the time, Pallas kernels for 0%

profile of v1, /device:TPU:0, one launch (start us, length us, event | category | flops | bytes accessed | tf_op | source)
XLA Modules:
  0.0 711.2 jit_solution(11976273718335008930)
XLA Ops:
  6.5 0.0 reduce-scatter.2.cloned.1.call-start
  6.5 0.5 collective-permute-start
  7.0 25.9 %collective-permute-done = bf16[1024,1024]{1,0:T(8,128)(2,1)S(1)} collective-permute-done((bf16[1024,1024]{1,0:T(8,128)(2,1)}, bf16[1024,1024]{1,0:T(8,128)(2,1)S(1)}, u32[]{:S(2)}, u32[]{:S(2)}) %collective-permute-start) | collective-permute-done | bytes 2097184 | tf_op jit(solution)/shard_map/ppermute | solution.py:17
  32.9 1.3 copy-done.1
  34.3 0.0 collective-permute-start.1
  34.3 25.6 %collective-permute-done.1 = bf16[1024,1024]{1,0:T(8,128)(2,1)} collective-permute-done((bf16[1024,1024]{1,0:T(8,128)(2,1)S(1)}, bf16[1024,1024]{1,0:T(8,128)(2,1)}, u32[]{:S(2)}, u32[]{:S(2)}) %collective-permute-start.1) | collective-permute-done | bytes 2097184 | tf_op jit(solution)/shard_map/ppermute | solution.py:17
  59.8 0.0 collective-permute-start.2
  59.8 25.8 %collective-permute-done.2 = bf16[1024,1024]{1,0:T(8,128)(2,1)} collective-permute-done((bf16[1024,1024]{1,0:T(8,128)(2,1)}, bf16[1024,1024]{1,0:T(8,128)(2,1)}, u32[]{:S(2)}, u32[]{:S(2)}) %collective-permute-start.2) | collective-permute-done | bytes 2097184 | tf_op jit(solution)/shard_map/ppermute | solution.py:17
  85.6 1.8 constant_dynamic-update-slice_fusion.7
  87.4 1.8 constant_dynamic-update-slice_fusion.6
  89.1 0.2 constant_dynamic-update-slice_fusion.5
  89.3 0.2 constant_dynamic-update-slice_fusion.4
  89.5 1.8 constant_dynamic-update-slice_fusion.3
  91.3 1.8 constant_dynamic-update-slice_fusion.2
  93.0 0.2 constant_dynamic-update-slice_fusion.1
  93.2 0.2 constant_dynamic-update-slice_fusion
  93.4 5.7 copy-done.3
  99.2 11.8 %fusion.2 = f32[4096,1024]{1,0:T(8,128)} fusion(bf16[1024,1024]{1,0:T(8,128)(2,1)S(1)} %copy-done, bf16[8192,1024]{1,0:T(8,128)(2,1)S(1)} %constant_dynamic-update-slice_fusion, s32[]{:T(128)S(6)} %select_n.14), kind=kOutput, calls=%fused_computation.2 | convolution fusion | flops 8589934592 | bytes 27262980 | tf_op jit(solution)/shard_map/dot_general | solution.py:22
  111.0 0.0 reduce-scatter.2.cloned.1.call-update
  111.0 0.0 all-gather.6.cloned.1.call-start
  111.0 282.3 %reduce-scatter.2.cloned.1.call-done = f32[512,1024]{1,0:T(8,128)} async-done(((f32[4096,1024]{1,0:T(8,128)}), f32[512,1024]{1,0:T(8,128)}) %reduce-scatter.2.cloned.1.call-update) | async-done | bytes 2097168 | tf_op jit(solution)/shard_map/reduce_scatter | solution.py:21
  393.3 2.7 convert_bitcast_fusion
  396.0 0.0 all-gather.6.cloned.1.call-update
  396.1 0.0 all-gather.4.cloned.1.call-start
  396.1 0.7 all-gather.4.cloned.1.call-update
  396.8 0.0 all-gather.8.cloned.1.call-start
  396.9 32.9 %all-gather.6.cloned.1.call-done = bf16[4096,512]{0,1:T(8,128)(2,1)} async-done(((bf16[1024,512]{0,1:T(8,128)(2,1)}), bf16[4096,512]{0,1:T(8,128)(2,1)}) %all-gather.6.cloned.1.call-update) | async-done | bytes 4194320 | tf_op jit(solution)/shard_map/all_gather | solution.py:30
  429.8 126.6 %all-gather.4.cloned.1.call-done = bf16[1024,4096]{0,1:T(8,128)(2,1)} async-done(((bf16[1024,512]{0,1:T(8,128)(2,1)}), bf16[1024,4096]{0,1:T(8,128)(2,1)}) %all-gather.4.cloned.1.call-update) | async-done | bytes 8388624 | tf_op jit(solution)/shard_map/all_gather | solution.py:33
  556.4 10.3 %add_convert_fusion = bf16[1024,512]{0,1:T(8,128)(2,1)} fusion(bf16[1024,512]{0,1:T(8,128)(2,1)} %convert_bitcast_fusion, bf16[4096,512]{0,1:T(8,128)(2,1)} %all-gather.6.cloned.1.call-done, bf16[1024,4096]{0,1:T(8,128)(2,1)} %all-gather.4.cloned.1.call-done), kind=kOutput, calls=%fused_computation.5 | convolution fusion | flops 4297588736 | bytes 14680064 | tf_op jit(solution)/shard_map/dot_general | solution.py:32
  566.7 0.0 all-gather.8.cloned.1.call-update
  566.7 122.8 %all-gather.8.cloned.1.call-done = bf16[1024,4096]{0,1:T(8,128)(2,1)} async-done(((bf16[1024,512]{0,1:T(8,128)(2,1)}), bf16[1024,4096]{0,1:T(8,128)(2,1)}) %all-gather.8.cloned.1.call-update) | async-done | bytes 8388624 | tf_op jit(solution)/shard_map/all_gather | solution.py:40
  689.5 15.1 %add_multiply_fusion = f32[1024,1024]{1,0:T(8,128)} fusion(bf16[1024,1024]{1,0:T(8,128)(2,1)S(1)} %copy-done, bf16[1024,4096]{0,1:T(8,128)(2,1)} %all-gather.8.cloned.1.call-done, bf16[8192,1024]{1,0:T(8,128)(2,1)} %copy-done.3, s32[]{:T(128)S(6)} %select_n.14), kind=kOutput, calls=%fused_computation.4 | convolution fusion | flops 8594128896 | bytes 23068676 | tf_op jit(solution)/shard_map/dot_general | solution.py:39
  (6 shorter events, 0.0 us)
Async XLA Ops:
  6.5 82.8 %copy-start = (bf16[1024,1024]{1,0:T(8,128)(2,1)S(1)}, bf16[1024,1024]{1,0:T(8,128)(2,1)}, u32[]{:S(2)}) copy-start(bf16[1024,1024]{1,0:T(8,128)(2,1)} %param.1) | copy-start | bytes 6291460
  6.5 386.8 %reduce-scatter.2.cloned.1.call-start = ((), (), s32[]{:S(2)}) async-start(), calls=%async_computation.1 | async-start | bytes 18874368 | tf_op jit(solution)/shard_map/reduce_scatter | solution.py:21
  6.5 26.4 %collective-permute-start = (bf16[1024,1024]{1,0:T(8,128)(2,1)}, bf16[1024,1024]{1,0:T(8,128)(2,1)S(1)}, u32[]{:S(2)}, u32[]{:S(2)}) collective-permute-start(bf16[1024,1024]{1,0:T(8,128)(2,1)} %param.1), channel_id=1, source_target_pairs={{0,8},{8,16},{16,24},{24,0},{1,9},{9,17},{17,25},{25,1},{2,10},{10... | collective-permute-start | bytes 6291464 | tf_op jit(solution)/shard_map/ppermute | solution.py:17
  32.9 1.3 copy-start.1
  34.3 25.6 %collective-permute-start.1 = (bf16[1024,1024]{1,0:T(8,128)(2,1)S(1)}, bf16[1024,1024]{1,0:T(8,128)(2,1)}, u32[]{:S(2)}, u32[]{:S(2)}) collective-permute-start(bf16[1024,1024]{1,0:T(8,128)(2,1)S(1)} %collective-permute-done), channel_id=1, source_target_pairs={{0,8},{8,16},{16,24},{24,0},{1,9},{9,17},{17,25},{25,1},{2,10},{10... | collective-permute-start | bytes 6291464 | tf_op jit(solution)/shard_map/ppermute | solution.py:17
  59.8 25.8 %collective-permute-start.2 = (bf16[1024,1024]{1,0:T(8,128)(2,1)}, bf16[1024,1024]{1,0:T(8,128)(2,1)}, u32[]{:S(2)}, u32[]{:S(2)}) collective-permute-start(bf16[1024,1024]{1,0:T(8,128)(2,1)} %collective-permute-done.1), channel_id=1, source_target_pairs={{0,8},{8,16},{16,24},{24,0},{1,9},{9,17},{17,25},{25,1},{2,10},{10... | collective-permute-start | bytes 6291464 | tf_op jit(solution)/shard_map/ppermute | solution.py:17
  59.8 29.3 %copy-start.2 = (bf16[1024,1024]{1,0:T(8,128)(2,1)S(1)}, bf16[1024,1024]{1,0:T(8,128)(2,1)}, u32[]{:S(2)}) copy-start(bf16[1024,1024]{1,0:T(8,128)(2,1)} %copy-done.1) | copy-start | bytes 6291460
  93.4 5.7 copy-start.3
  111.0 318.8 %all-gather.6.cloned.1.call-start = ((), (), s32[]{:S(2)}) async-start(), calls=%async_computation.3 | async-start | bytes 5242880 | tf_op jit(solution)/shard_map/all_gather | solution.py:30
  396.1 160.3 %all-gather.4.cloned.1.call-start = ((), (), s32[]{:S(2)}) async-start(), calls=%async_computation.2 | async-start | bytes 9437184 | tf_op jit(solution)/shard_map/all_gather | solution.py:33
  396.8 292.7 %all-gather.8.cloned.1.call-start = ((), (), s32[]{:S(2)}) async-start(), calls=%async_computation.4 | async-start | bytes 9437184 | tf_op jit(solution)/shard_map/all_gather | solution.py:40
Sparse Core Ops, SparseCore 0:
  111.1 282.1 reduce-scatter.1
  396.2 33.5 all-gather.5
  431.9 124.4 all-gather.3
  566.9 122.6 all-gather.7
